TPU v7x, 256 devices: a whole 4x4x8 slice. The times are simulated.
256 devices in a mesh: island: 8 (over y, x_lo), fsdp: 32 (over z, x_hi, core).
Axes of the slice: x: 4 (x_hi: 2, x_lo: 2; x = x_hi * 2 + x_lo), y: 4, z: 8, core: 2. Of those that a mesh axis runs over, the one named last changes fastest.
Arguments:
- tokens: bfloat16 [65536, 4096], P(('island', 'fsdp')), may hold values from -6 to 6
- upstream: bfloat16 [65536, 1024], P(('island', 'fsdp')), may hold values from -6 to 6
- params: float32 [4096, 1024], P('fsdp'), may hold values from -6 to 6
- momentum: float32 [4096, 1024], P('fsdp'), may hold values from -4 to 4
- projection: float32 [1024, 512], replicated, may hold values from -6 to 6
Outputs:
- values: bfloat16 [65536, 1024], P(('island', 'fsdp'))
- token_grads: bfloat16 [65536, 4096], P(('island', 'fsdp'))
- new_params: float32 [4096, 1024], P('fsdp')
- new_momentum: float32 [4096, 1024], P('fsdp')
All inputs are finite; a program needn't handle non-finite values.
Results may differ from a plain program's by a relative error of at most 0.012.
Values may be sent and summed in bfloat16 or wider, within the bound.
No kernel may reach another device: no remote copies, remote signals or barrier semaphores. Data moves between devices by JAX's collectives and lax.ppermute only.
A program may use at most 128 MiB of HBM per device.

v0:
```python
import math
import jax
import jax.numpy as jnp
from jax import lax
from jax.sharding import PartitionSpec as P


def local(tokens, upstream, params, momentum, projection):
    half_weight = params.astype(jnp.bfloat16)
    inv_width = 1.0 / math.sqrt(tokens.shape[1])
    dims_feat = (((1,), (1,)), ((), ()))
    dims_rows = (((0,), (0,)), ((), ()))
    forward_sum = jnp.dot(
        tokens,
        lax.all_gather(half_weight, "fsdp", axis=0, tiled=True),
        preferred_element_type=jnp.float32,
    )
    product = lax.dot_general(
        upstream,
        lax.all_gather(half_weight, "fsdp", axis=0, tiled=True),
        dims_feat,
        preferred_element_type=jnp.float32,
    )
    token_grads = (product * inv_width).astype(jnp.bfloat16)
    values = (forward_sum * inv_width).astype(jnp.bfloat16)
    fsdp_count = lax.axis_size("fsdp")
    scale_tok = 1.0 / math.sqrt(tokens.shape[0] * fsdp_count)
    local_grad = lax.dot_general(tokens, upstream, dims_rows, preferred_element_type=jnp.float32)
    shard_grad = lax.psum_scatter(local_grad, "fsdp", scatter_dimension=0, tiled=True) * scale_tok
    compressed = jnp.dot(shard_grad, projection, precision=lax.Precision.HIGHEST)
    island_total = lax.psum(compressed.astype(jnp.bfloat16), "island").astype(jnp.float32)
    outer = jnp.dot(island_total, projection.T, precision=lax.Precision.HIGHEST) / (
        projection.shape[1] * lax.axis_size("island")
    )
    new_momentum = 0.9 * momentum + outer
    new_params = params - 0.7 * (outer + 0.9 * new_momentum)
    return (values, token_grads, new_params, new_momentum)


def solution(mesh):
    in_specs = (
        P(("island", "fsdp"), None),
        P(("island", "fsdp"), None),
        P("fsdp", None),
        P("fsdp", None),
        P(),
    )
    out_specs = (
        P(("island", "fsdp"), None),
        P(("island", "fsdp"), None),
        P("fsdp", None),
        P("fsdp", None),
    )
    return jax.shard_map(local, mesh=mesh, in_specs=in_specs, out_specs=out_specs, check_vma=False)
```

profile of v0, /device:TPU:1, one launch (start us, length us, event | category | flops | bytes accessed | tf_op | source)
XLA Modules:
  0.0 444.7 jit_solution(7758417855345706923)
XLA Ops:
  7.2 0.0 copy-start
  7.2 0.0 reduce-scatter.2.cloned.1.call-start
  7.2 1.5 copy-done
  8.8 9.2 %fusion.5 = f32[4096,1024]{1,0:T(8,128)} fusion(bf16[256,4096]{1,0:T(8,128)(2,1)S(1)} %copy-done, bf16[256,1024]{1,0:T(8,128)(2,1)} %param.6), kind=kOutput, calls=%fused_computation.11 | convolution fusion | flops 2147483648 | bytes 19398656 | tf_op jit(solution)/shard_map/dot_general | solution.py:28
  17.9 0.0 reduce-scatter.2.cloned.1.call-update
  17.9 0.0 copy-start.1
  18.0 0.0 copy-start.2
  18.0 0.0 all-reduce.2.cloned.1.call-start
  18.0 219.4 %reduce-scatter.2.cloned.1.call-done = f32[128,1024]{1,0:T(8,128)} async-done(((f32[4096,1024]{1,0:T(8,128)}), f32[128,1024]{1,0:T(8,128)}) %reduce-scatter.2.cloned.1.call-update) | async-done | bytes 524304 | tf_op jit(solution)/shard_map/reduce_scatter | solution.py:29
  237.4 3.7 convolution_convert_fusion
  241.1 0.0 all-reduce.2.cloned.1.call-update
  241.1 0.0 all-gather.2.cloned.1.call-start
  241.2 76.1 %all-reduce.2.cloned.1.call-done = bf16[128,512]{1,0:T(8,128)(2,1)} async-done(((bf16[128,512]{1,0:T(8,128)(2,1)}), bf16[128,512]{1,0:T(8,128)(2,1)}) %all-reduce.2.cloned.1.call-update) | async-done | bytes 131088 | tf_op jit(solution)/shard_map/psum | solution.py:31
  317.3 0.0 copy-done.1
  317.3 0.0 copy-done.2
  317.3 4.0 multiply_subtract_fusion
  321.3 0.0 all-gather.2.cloned.1.call-update
  321.4 0.0 copy-start.3
  321.4 106.3 %all-gather.2.cloned.1.call-done = bf16[4096,1024]{1,0:T(8,128)(2,1)} async-done(((bf16[128,1024]{1,0:T(8,128)(2,1)}), bf16[4096,1024]{1,0:T(8,128)(2,1)}) %all-gather.2.cloned.1.call-update) | async-done | bytes 8388624 | tf_op jit(solution)/shard_map/all_gather | solution.py:15
  427.7 0.0 copy-start.4
  427.7 6.7 %fusion.1 = bf16[256,1024]{1,0:T(8,128)(2,1)} fusion(bf16[256,4096]{1,0:T(8,128)(2,1)S(1)} %copy-done, bf16[4096,1024]{1,0:T(8,128)(2,1)} %all-gather.2.cloned.1.call-done), kind=kOutput, calls=%fused_computation.3 | convolution fusion | flops 2148007936 | bytes 11010048 | tf_op jit(solution)/shard_map/dot_general | solution.py:13
  434.4 0.0 copy-done.3
  434.4 0.0 copy-done.4
  434.4 3.8 fusion
Async XLA Ops:
  7.2 1.6 copy-start
  7.2 230.2 %reduce-scatter.2.cloned.1.call-start = ((), (), s32[]{:S(2)}) async-start(), calls=%async_computation.2 | async-start | bytes 17301504 | tf_op jit(solution)/shard_map/reduce_scatter | solution.py:29
  17.9 299.3 %copy-start.1 = (f32[128,1024]{1,0:T(8,128)S(1)}, f32[128,1024]{1,0:T(8,128)}, u32[]{:S(2)}) copy-start(f32[128,1024]{1,0:T(8,128)} %param.7) | copy-start | bytes 1572868
  18.0 299.3 %copy-start.2 = (f32[128,1024]{1,0:T(8,128)S(1)}, f32[128,1024]{1,0:T(8,128)}, u32[]{:S(2)}) copy-start(f32[128,1024]{1,0:T(8,128)} %param.8) | copy-start | bytes 1572868
  18.0 299.3 %all-reduce.2.cloned.1.call-start = ((), (), s32[]{:S(2)}) async-start(), calls=%async_computation.3 | async-start | bytes 262144 | tf_op jit(solution)/shard_map/psum | solution.py:31
  241.1 186.6 %all-gather.2.cloned.1.call-start = ((), (), s32[]{:S(2)}) async-start(), calls=%async_computation.1 | async-start | bytes 8650752 | tf_op jit(solution)/shard_map/all_gather | solution.py:15
  321.4 113.0 %copy-start.3 = (bf16[256,1024]{1,0:T(8,128)(2,1)S(1)}, bf16[256,1024]{1,0:T(8,128)(2,1)}, u32[]{:S(2)}) copy-start(bf16[256,1024]{1,0:T(8,128)(2,1)} %param.6) | copy-start | bytes 1572868
  427.7 6.7 %copy-start.4 = (bf16[4096,1024]{1,0:T(8,128)(2,1)S(1)}, bf16[4096,1024]{1,0:T(8,128)(2,1)}, u32[]{:S(2)}) copy-start(bf16[4096,1024]{1,0:T(8,128)(2,1)} %all-gather.2.cloned.1.call-done) | copy-start | bytes 25165828
Sparse Core Ops, SparseCore 0:
  18.1 219.2 reduce-scatter.1
  241.3 75.9 all-reduce.1
  321.5 106.1 all-gather.1
where the time goes:
time: 445 us
  waiting for transfers between devices  402 us (90%)
  matrix products  27.4 us (6%)
  between operations  13.8 us (3%)
    reduce_scatter x1, waiting for transfers between devices, local(): lax.psum_scatter(local_grad, 'fsdp', scatter_dimension=0, tiled=True)  219 us
    all_gather x1, waiting for transfers between devices, local(): lax.all_gather(half_weight, 'fsdp', axis=0, tiled=True)  106 us
    psum x1, waiting for transfers between devices, local(): lax.psum(compressed.astype(jnp.bfloat16), 'island').astype(jnp.float32)  76.1 us
    dot_general x1, matrix products, local(): lax.dot_general(tokens, upstream, dims_rows, preferred_element_type=jnp.f...  9.16 us
  transfers between devices with their start and end apart: 3, of which 3 were waited for; matrix products, arithmetic and copies ran while one was open for 0% of the time, Pallas kernels for 0%

commit v1 on v0

--- a/solution.py
+++ b/solution.py
@@ -10,10 +10,18 @@
     inv_width = 1.0 / math.sqrt(tokens.shape[1])
     dims_feat = (((1,), (1,)), ((), ()))
     dims_rows = (((0,), (0,)), ((), ()))
+
+    def feed_results_here(piece_in, mesh_ax):
+        current_block = jnp.concatenate(
+            jax.lax.all_to_all(
+                jnp.stack([piece_in] * jax.lax.axis_size(mesh_ax), axis=0), mesh_ax, 0, 0
+            ),
+            axis=0,
+        )
+        return current_block
+
     forward_sum = jnp.dot(
-        tokens,
-        lax.all_gather(half_weight, "fsdp", axis=0, tiled=True),
-        preferred_element_type=jnp.float32,
+        tokens, feed_results_here(half_weight, "fsdp"), preferred_element_type=jnp.float32
     )
     product = lax.dot_general(
         upstream,

time: 445 us -> 575 us (1.29)
  waiting for transfers between devices: 402 us -> 507 us
  starting transfers between devices: 0.12 us -> 15.3 us
    all_to_all x0 -> x1, waiting for transfers between devices: none -> 211 us  [feed_results_here(): jax.lax.all_to_all(jnp.stack([piece_in] * jax.lax.axis_size(mesh_ax), axi...]
    all_gather x1, waiting for transfers between devices: 106 us -> 0.01 us  [local(): lax.all_gather(half_weight, 'fsdp', axis=0, tiled=True)]
    all_to_all x0 -> x1, starting transfers between devices: none -> 15.2 us  [feed_results_here(): jax.lax.all_to_all(jnp.stack([piece_in] * jax.lax.axis_size(mesh_ax), axi...]
  transfers between devices with their start and end apart: 3 -> 4, of which waited for: 3 -> 3; matrix products, arithmetic and copies ran while one was open for 0% -> 1% of each run, Pallas kernels for 0% -> 0%
where the time goes in v1:
time: 575 us; the launch traced here: 573 us
  waiting for transfers between devices  507 us (88%)
  matrix products  30.5 us (5%)
  starting transfers between devices  15.3 us (3%)
  between operations  13.8 us (2%)
  local copies, waits for them, and re-layouts  5.85 us (1%)
    reduce_scatter x1, waiting for transfers between devices, local(): lax.psum_scatter(local_grad, 'fsdp', scatter_dimension=0, tiled=True)  219 us
    all_to_all x1, waiting for transfers between devices, feed_results_here(): jax.lax.all_to_all(jnp.stack([piece_in] * jax.lax.axis_size(mesh_ax), axi...  211 us
    psum x1, waiting for transfers between devices, local(): lax.psum(compressed.astype(jnp.bfloat16), 'island').astype(jnp.float32)  76.1 us
    all_to_all x1, starting transfers between devices, feed_results_here(): jax.lax.all_to_all(jnp.stack([piece_in] * jax.lax.axis_size(mesh_ax), axi...  15.2 us
  transfers between devices with their start and end apart: 4, of which 3 were waited for; matrix products, arithmetic and copies ran while one was open for 1% of the time, Pallas kernels for 0%

profile of v1, /device:TPU:1, one launch (start us, length us, event | category | flops | bytes accessed | tf_op | source)
XLA Modules:
  0.0 573.0 jit_solution(2527498018438119255)
XLA Ops:
  7.2 0.0 copy-start
  7.2 0.0 reduce-scatter.2.cloned.1.call-start
  7.2 1.5 copy-done
  8.8 9.2 %fusion.5 = f32[4096,1024]{1,0:T(8,128)} fusion(bf16[256,4096]{1,0:T(8,128)(2,1)S(1)} %copy-done, bf16[256,1024]{1,0:T(8,128)(2,1)} %param.6), kind=kOutput, calls=%fused_computation.11 | convolution fusion | flops 2147483648 | bytes 19398656 | tf_op jit(solution)/shard_map/dot_general | solution.py:36
  17.9 0.0 reduce-scatter.2.cloned.1.call-update
  18.0 0.0 copy-start.2
  18.0 0.0 copy-start.3
  18.0 0.0 all-reduce.2.cloned.1.call-start
  18.0 219.4 %reduce-scatter.2.cloned.1.call-done = f32[128,1024]{1,0:T(8,128)} async-done(((f32[4096,1024]{1,0:T(8,128)}), f32[128,1024]{1,0:T(8,128)}) %reduce-scatter.2.cloned.1.call-update) | async-done | bytes 524304 | tf_op jit(solution)/shard_map/reduce_scatter | solution.py:37
  237.4 3.7 convolution_convert_fusion
  241.1 0.0 all-reduce.2.cloned.1.call-update
  241.2 76.1 %all-reduce.2.cloned.1.call-done = bf16[128,512]{1,0:T(8,128)(2,1)} async-done(((bf16[128,512]{1,0:T(8,128)(2,1)}), bf16[128,512]{1,0:T(8,128)(2,1)}) %all-reduce.2.cloned.1.call-update) | async-done | bytes 131088 | tf_op jit(solution)/shard_map/psum | solution.py:39
  317.3 0.0 copy-done.2
  317.3 0.0 copy-done.3
  317.3 4.0 multiply_subtract_fusion
  321.3 0.0 copy-start.1
  321.3 4.3 stack.2
  325.6 0.0 copy-done.1
  325.6 15.2 %all-to-all-start = ((bf16[32,128,1024]{2,1,0:T(8,128)(2,1)}), bf16[32,128,1024]{2,1,0:T(8,128)(2,1)}, u32[]{:S(2)}, u32[]{:S(2)}) async-start(bf16[32,128,1024]{2,1,0:T(8,128)(2,1)} %stack.2), calls=%async_computation | async-start | bytes 16777216 | tf_op jit(solution)/shard_map/all_to_all | solution.py:16
  340.8 0.0 all-gather.2.cloned.1.call-start
  340.8 0.7 all-gather.2.cloned.1.call-update
  341.5 211.3 %all-to-all-done = bf16[32,128,1024]{2,1,0:T(8,128)(2,1)} async-done(((bf16[32,128,1024]{2,1,0:T(8,128)(2,1)}), bf16[32,128,1024]{2,1,0:T(8,128)(2,1)}, u32[]{:S(2)}, u32[]{:S(2)}) %all-to-all-start) | async-done | bytes 8388640 | tf_op jit(solution)/shard_map/all_to_all | solution.py:16
  552.8 0.0 copy-start.4
  552.8 6.6 %fusion.1 = bf16[256,1024]{1,0:T(8,128)(2,1)} fusion(bf16[256,4096]{1,0:T(8,128)(2,1)S(1)} %copy-done, bf16[4096,1024]{1,0:T(8,128)(2,1)} %bitcast), kind=kOutput, calls=%fused_computation.3 | convolution fusion | flops 2148007936 | bytes 11010048 | tf_op jit(solution)/shard_map/dot_general | solution.py:23
  559.4 0.0 all-gather.2.cloned.1.call-done
  559.4 0.0 copy-done.4
  559.4 7.1 %fusion = bf16[256,4096]{1,0:T(8,128)(2,1)} fusion(bf16[256,1024]{1,0:T(8,128)(2,1)S(1)} %copy-done.4, bf16[4096,1024]{1,0:T(8,128)(2,1)} %all-gather.2.cloned.1.call-done), kind=kOutput, calls=%fused_computation.1 | convolution fusion | flops 2149580800 | bytes 11010048 | tf_op jit(solution)/shard_map/dot_general | solution.py:26
Async XLA Ops:
  7.2 1.6 copy-start
  7.2 230.2 %reduce-scatter.2.cloned.1.call-start = ((), (), s32[]{:S(2)}) async-start(), calls=%async_computation.3 | async-start | bytes 17301504 | tf_op jit(solution)/shard_map/reduce_scatter | solution.py:37
  18.0 299.3 %copy-start.2 = (f32[128,1024]{1,0:T(8,128)S(1)}, f32[128,1024]{1,0:T(8,128)}, u32[]{:S(2)}) copy-start(f32[128,1024]{1,0:T(8,128)} %param.7) | copy-start | bytes 1572868
  18.0 299.3 %copy-start.3 = (f32[128,1024]{1,0:T(8,128)S(1)}, f32[128,1024]{1,0:T(8,128)}, u32[]{:S(2)}) copy-start(f32[128,1024]{1,0:T(8,128)} %param.8) | copy-start | bytes 1572868
  18.0 299.3 %all-reduce.2.cloned.1.call-start = ((), (), s32[]{:S(2)}) async-start(), calls=%async_computation.4 | async-start | bytes 262144 | tf_op jit(solution)/shard_map/psum | solution.py:39
  321.3 4.3 copy-start.1
  325.6 227.2 %all-to-all-start = ((bf16[32,128,1024]{2,1,0:T(8,128)(2,1)}), bf16[32,128,1024]{2,1,0:T(8,128)(2,1)}, u32[]{:S(2)}, u32[]{:S(2)}) async-start(bf16[32,128,1024]{2,1,0:T(8,128)(2,1)} %stack.2), calls=%async_computation | async-start | bytes 16777216 | tf_op jit(solution)/shard_map/all_to_all | solution.py:16
  340.8 218.6 %all-gather.2.cloned.1.call-start = ((), (), s32[]{:S(2)}) async-start(), calls=%async_computation.2 | async-start | bytes 8650752 | tf_op jit(solution)/shard_map/all_gather | solution.py:28
  552.8 6.6 %copy-start.4 = (bf16[256,1024]{1,0:T(8,128)(2,1)S(1)}, bf16[256,1024]{1,0:T(8,128)(2,1)}, u32[]{:S(2)}) copy-start(bf16[256,1024]{1,0:T(8,128)(2,1)} %param.6) | copy-start | bytes 1572868
Sparse Core Ops, SparseCore 0:
  18.1 219.2 reduce-scatter.1
  241.3 75.9 all-reduce.1
  345.0 162.2 all-gather.1

commit v2 on v0

--- a/solution.py
+++ b/solution.py
@@ -3,6 +3,8 @@
 import jax.numpy as jnp
 from jax import lax
 from jax.sharding import PartitionSpec as P
+
+launch_values = lambda a0, peer_axis: jax.lax.all_gather(a0, peer_axis).sum(axis=0)
 
 
 def local(tokens, upstream, params, momentum, projection):
@@ -28,7 +30,7 @@
     local_grad = lax.dot_general(tokens, upstream, dims_rows, preferred_element_type=jnp.float32)
     shard_grad = lax.psum_scatter(local_grad, "fsdp", scatter_dimension=0, tiled=True) * scale_tok
     compressed = jnp.dot(shard_grad, projection, precision=lax.Precision.HIGHEST)
-    island_total = lax.psum(compressed.astype(jnp.bfloat16), "island").astype(jnp.float32)
+    island_total = launch_values(compressed.astype(jnp.bfloat16), "island").astype(jnp.float32)
     outer = jnp.dot(island_total, projection.T, precision=lax.Precision.HIGHEST) / (
         projection.shape[1] * lax.axis_size("island")
     )

time: 445 us -> 410 us (0.921)
  waiting for transfers between devices: 402 us -> 366 us
    psum x1 -> x0, waiting for transfers between devices: 76.1 us -> none  [local(): lax.psum(compressed.astype(jnp.bfloat16), 'island').astype(jnp.float32)]
    all_gather x0 -> x1, waiting for transfers between devices: none -> 40.1 us  [jax.lax.all_gather(a0, peer_axis).sum(axis=0)]
where the time goes in v2:
time: 410 us
  waiting for transfers between devices  366 us (89%)
  matrix products  27.3 us (7%)
  between operations  13.8 us (3%)
    reduce_scatter x1, waiting for transfers between devices, local(): lax.psum_scatter(local_grad, 'fsdp', scatter_dimension=0, tiled=True)  219 us
    all_gather x1, waiting for transfers between devices, local(): lax.all_gather(half_weight, 'fsdp', axis=0, tiled=True)  106 us
    all_gather x1, waiting for transfers between devices, jax.lax.all_gather(a0, peer_axis).sum(axis=0)  40.1 us
    dot_general x1, matrix products, local(): lax.dot_general(tokens, upstream, dims_rows, preferred_element_type=jnp.f...  9.16 us
  transfers between devices with their start and end apart: 3, of which 3 were waited for; matrix products, arithmetic and copies ran while one was open for 0% of the time, Pallas kernels for 0%

profile of v2, /device:TPU:1, one launch (start us, length us, event | category | flops | bytes accessed | tf_op | source)
XLA Modules:
  0.0 410.0 jit_solution(4446546454156979347)
XLA Ops:
  7.2 0.0 copy-start
  7.2 0.0 reduce-scatter.2.cloned.1.call-start
  7.2 1.5 copy-done
  8.8 9.2 %fusion.5 = f32[4096,1024]{1,0:T(8,128)} fusion(bf16[256,4096]{1,0:T(8,128)(2,1)S(1)} %copy-done, bf16[256,1024]{1,0:T(8,128)(2,1)} %param.6), kind=kOutput, calls=%fused_computation.11 | convolution fusion | flops 2147483648 | bytes 19398656 | tf_op jit(solution)/shard_map/dot_general | solution.py:30
  17.9 0.0 reduce-scatter.2.cloned.1.call-update
  17.9 0.0 copy-start.1
  18.0 0.0 copy-start.2
  18.0 0.0 all-gather.6.cloned.1.call-start
  18.0 219.4 %reduce-scatter.2.cloned.1.call-done = f32[128,1024]{1,0:T(8,128)} async-done(((f32[4096,1024]{1,0:T(8,128)}), f32[128,1024]{1,0:T(8,128)}) %reduce-scatter.2.cloned.1.call-update) | async-done | bytes 524304 | tf_op jit(solution)/shard_map/reduce_scatter | solution.py:31
  237.4 3.7 convolution_convert_fusion
  241.1 0.0 all-gather.6.cloned.1.call-update
  241.1 0.0 all-gather.4.cloned.1.call-start
  241.2 40.1 %all-gather.6.cloned.1.call-done = bf16[1024,512]{1,0:T(8,128)(2,1)} async-done(((bf16[128,512]{1,0:T(8,128)(2,1)}), bf16[1024,512]{1,0:T(8,128)(2,1)}) %all-gather.6.cloned.1.call-update) | async-done | bytes 1048592 | tf_op jit(solution)/shard_map/all_gather | solution.py:7
  281.3 1.4 reduce_sum.12
  282.6 0.0 copy-done.1
  282.7 0.0 copy-done.2
  282.7 4.0 multiply_subtract_fusion
  286.6 0.0 all-gather.4.cloned.1.call-update
  286.7 0.0 copy-start.3
  286.7 106.4 %all-gather.4.cloned.1.call-done = bf16[4096,1024]{1,0:T(8,128)(2,1)} async-done(((bf16[128,1024]{1,0:T(8,128)(2,1)}), bf16[4096,1024]{1,0:T(8,128)(2,1)}) %all-gather.4.cloned.1.call-update) | async-done | bytes 8388624 | tf_op jit(solution)/shard_map/all_gather | solution.py:17
  393.0 0.0 copy-start.4
  393.0 6.7 %fusion.1 = bf16[256,1024]{1,0:T(8,128)(2,1)} fusion(bf16[256,4096]{1,0:T(8,128)(2,1)S(1)} %copy-done, bf16[4096,1024]{1,0:T(8,128)(2,1)} %all-gather.4.cloned.1.call-done), kind=kOutput, calls=%fused_computation.3 | convolution fusion | flops 2148007936 | bytes 11010048 | tf_op jit(solution)/shard_map/dot_general | solution.py:15
  399.7 0.0 copy-done.3
  399.7 0.0 copy-done.4
  399.7 3.8 fusion
Async XLA Ops:
  7.2 1.6 copy-start
  7.2 230.2 %reduce-scatter.2.cloned.1.call-start = ((), (), s32[]{:S(2)}) async-start(), calls=%async_computation.2 | async-start | bytes 17301504 | tf_op jit(solution)/shard_map/reduce_scatter | solution.py:31
  17.9 264.7 %copy-start.1 = (f32[128,1024]{1,0:T(8,128)S(1)}, f32[128,1024]{1,0:T(8,128)}, u32[]{:S(2)}) copy-start(f32[128,1024]{1,0:T(8,128)} %param.7) | copy-start | bytes 1572868
  18.0 264.7 %copy-start.2 = (f32[128,1024]{1,0:T(8,128)S(1)}, f32[128,1024]{1,0:T(8,128)}, u32[]{:S(2)}) copy-start(f32[128,1024]{1,0:T(8,128)} %param.8) | copy-start | bytes 1572868
  18.0 263.3 %all-gather.6.cloned.1.call-start = ((), (), s32[]{:S(2)}) async-start(), calls=%async_computation.3 | async-start | bytes 1179648 | tf_op jit(solution)/shard_map/all_gather | solution.py:7
  241.1 151.9 %all-gather.4.cloned.1.call-start = ((), (), s32[]{:S(2)}) async-start(), calls=%async_computation.1 | async-start | bytes 8650752 | tf_op jit(solution)/shard_map/all_gather | solution.py:17
  286.7 113.0 %copy-start.3 = (bf16[256,1024]{1,0:T(8,128)(2,1)S(1)}, bf16[256,1024]{1,0:T(8,128)(2,1)}, u32[]{:S(2)}) copy-start(bf16[256,1024]{1,0:T(8,128)(2,1)} %param.6) | copy-start | bytes 1572868
  393.0 6.7 %copy-start.4 = (bf16[4096,1024]{1,0:T(8,128)(2,1)S(1)}, bf16[4096,1024]{1,0:T(8,128)(2,1)}, u32[]{:S(2)}) copy-start(bf16[4096,1024]{1,0:T(8,128)(2,1)} %all-gather.4.cloned.1.call-done) | copy-start | bytes 25165828
Sparse Core Ops, SparseCore 0:
  18.1 219.2 reduce-scatter.1
  241.3 39.9 all-gather.5
  286.8 106.2 all-gather.3
